TPU v7x, 32 devices: a whole 2x2x4 slice. The times are simulated.
32 devices in a mesh: dp: 8 (over z, y), tensor: 4 (over x, core).
Axes of the slice: x: 2, y: 2, z: 4, core: 2. Of those that a mesh axis runs over, the one named last changes fastest.
Arguments:
- tokens: bfloat16 [512, 1536], P('dp'), may hold values from -6 to 6
- norm_gain: float32 [1536], replicated, may hold values from 0.1 to 1.9
- w_query: bfloat16 [1536, 1024], P(None, 'tensor'), may hold values from -0.15625 to 0.15625
- w_keyval: bfloat16 [1536, 256], replicated, may hold values from -0.15625 to 0.15625
- w_out: bfloat16 [1024, 1536], P('tensor'), may hold values from -0.5 to 0.5
- kv_pool: bfloat16 [4096, 128, 256], P(('dp', 'tensor')), may hold values from -256 to 256
- page_table: int32 [512, 8], P('dp', 'tensor'), may hold values from 0 to 127, as said below
- positions: int32 [512], P('dp'), may hold values from 0 to 8191
- assignment: int32 [512], P('dp'), may hold values from 0 to 511, as said below
Outputs:
- attn_out: bfloat16 [512, 1536], P('dp')
Inputs may be any that keep to these rules, and one draw needn't show every extreme that they name: `assignment`: the serving slot is the serving device's dp index times 64 plus a local slot; each serving slot is taken by exactly one request; the 64 requests of one device go to 8 distinct devices, exactly 8 to each. `page_table`: on each device the entries form a permutation of 0 to 127.
All inputs are finite; a program needn't handle non-finite values.
Results may differ from a plain program's by a relative error of at most 0.03.
Values may be sent and summed in bfloat16 or wider, within the bound.
A program may use at most 64 MiB of HBM per device.

v0:
```python
import jax
import jax.numpy as jnp
from jax import lax
from jax.sharding import PartitionSpec as P

masked_score = -1e30
norm_eps = 1e-06
rotary_base = 10000.0


def combined_all(array, axis, join):
    gathered = jax.tree.map(
        lambda a, kind: lax.all_gather(a.astype(kind), axis),
        array,
        (jnp.bfloat16, jnp.bfloat16, jnp.bfloat16),
    )

    def take(source):
        return jax.tree.map(
            lambda a, own: lax.dynamic_index_in_dim(a, source, 0, False).astype(own.dtype),
            gathered,
            array,
        )

    return lax.fori_loop(
        1, lax.axis_size(axis), lambda source, state: join(state, take(source)), take(0)
    )


def as_sent(array):

    def short(part):
        return part.astype(jnp.bfloat16) if part.dtype == jnp.float32 else part

    return jax.tree.map(short, array)


def rotate(values, where, width):
    half = width // 2
    freqs = rotary_base ** (-jnp.arange(half, dtype=jnp.float32) * 2.0 / width)
    angles = where.astype(jnp.float32)[..., None] * freqs
    cosine = jnp.cos(angles)
    sine = jnp.sin(angles)
    first = values[..., :half]
    second = values[..., half:]
    return jnp.concatenate(
        [first * cosine - second * sine, first * sine + second * cosine], axis=-1
    )


def combine_stats(first, second):
    peak = jnp.maximum(first[0], second[0])
    first_scale = jnp.exp(first[0] - peak)
    second_scale = jnp.exp(second[0] - peak)
    total = first[1] * first_scale + second[1] * second_scale
    summed = first[2] * first_scale[..., None] + second[2] * second_scale[..., None]
    return (peak, total, summed)


def local(tokens, norm_gain, w_query, w_keyval, w_out, kv_pool, page_table, positions, assignment):
    head_width = w_keyval.shape[1] // 2
    row_count = tokens.shape[0]
    group_size = lax.axis_size("tensor")
    data_size = lax.axis_size("dp")
    local_heads = w_query.shape[1] // head_width
    all_heads = local_heads * group_size
    capacity = max(2, row_count // data_size)
    slots_all = data_size * capacity
    scale = head_width ** (-0.5)
    here = lax.axis_index("tensor")
    floats = tokens.astype(jnp.float32)
    normed = (
        floats * lax.rsqrt(jnp.mean(floats * floats, axis=-1, keepdims=True) + norm_eps) * norm_gain
    ).astype(jnp.bfloat16)
    query = jnp.dot(normed, w_query, preferred_element_type=jnp.float32).reshape(
        row_count, local_heads, head_width
    )
    query = rotate(query, positions[:, None], head_width).astype(jnp.bfloat16)
    key_value = jnp.dot(normed, w_keyval, preferred_element_type=jnp.float32)
    new_key = rotate(key_value[:, :head_width], positions, head_width).astype(jnp.bfloat16)
    new_value = key_value[:, head_width:].astype(jnp.bfloat16)
    target = assignment // row_count
    local_slot = assignment % row_count
    hits = (target[:, None] == jnp.arange(data_size, dtype=jnp.int32)[None, :]).astype(jnp.int32)
    order_in = jnp.sum(jnp.cumsum(hits, axis=0) * hits, axis=1) - 1
    place = target * capacity + order_in

    def to_buffer(values):
        empty = jnp.zeros((slots_all,) + values.shape[1:], values.dtype)
        filled = empty.at[place].set(values)
        return filled.reshape((data_size, capacity) + values.shape[1:])

    def source_buffer(values):
        return values.reshape((slots_all,) + values.shape[2:])[place]

    tags = to_buffer(jnp.stack([positions, local_slot + 1], axis=1))
    tags = lax.all_to_all(tags, "dp", split_axis=0, concat_axis=0, tiled=True).reshape(slots_all, 2)
    served_slot = tags[:, 1] - 1
    scatter_slot = jnp.where(served_slot < 0, row_count, served_slot)
    gather_slot = jnp.maximum(served_slot, 0)

    def compact(values):
        empty = jnp.zeros((row_count,) + values.shape[1:], values.dtype)
        return empty.at[scatter_slot].set(values, mode="drop")

    def expand(values):
        return values[gather_slot].reshape((data_size, capacity) + values.shape[1:])

    current = compact(tags[:, 0])
    full_query = lax.all_gather(query, "tensor", axis=1, tiled=True)
    served_heads = lax.all_to_all(
        to_buffer(full_query), "dp", split_axis=0, concat_axis=0, tiled=True
    )
    served_heads = compact(served_heads.reshape(slots_all, all_heads, head_width))
    page_rows = page_table.shape[1]
    page_len = kv_pool.shape[1]
    window = page_rows * group_size * page_len
    page_entries = kv_pool[page_table].reshape(row_count, page_rows * page_len, 2 * head_width)
    scores = (
        jnp.einsum(
            "vto,vio->vti",
            served_heads,
            page_entries[..., :head_width],
            preferred_element_type=jnp.float32,
        )
        * scale
    )
    cycle_slot = here * page_rows * page_len + jnp.arange(page_rows * page_len, dtype=jnp.int32)
    offset = jnp.mod(cycle_slot[None, :] - current[:, None], window)
    valid = ((offset != 0) & (current[:, None] - window + offset >= 0))[:, None, :]
    peak = jnp.max(jnp.where(valid, scores, masked_score), axis=2)
    weight_tensors = jnp.where(valid, jnp.exp(scores - peak[..., None]), 0.0)
    total = jnp.sum(weight_tensors, axis=2)
    summed = jnp.einsum(
        "rbi,ril->rbl",
        weight_tensors.astype(jnp.bfloat16),
        page_entries[..., head_width:],
        preferred_element_type=jnp.float32,
    )
    merged = combined_all((peak, total, summed), "tensor", combine_stats)
    returned = (
        lax.all_to_all(as_sent(expand(merged[0])), "dp", split_axis=0, concat_axis=0, tiled=True),
        lax.all_to_all(as_sent(expand(merged[1])), "dp", split_axis=0, concat_axis=0, tiled=True),
        lax.all_to_all(as_sent(expand(merged[2])), "dp", split_axis=0, concat_axis=0, tiled=True),
    )
    own_stats = tuple(
        (
            lax.dynamic_slice_in_dim(source_buffer(member), here * local_heads, local_heads, 1)
            for member in returned
        )
    )
    cache_peak, cache_total, cache_summed = own_stats
    self_score = (
        jnp.einsum("rhd,rd->rh", query, new_key, preferred_element_type=jnp.float32) * scale
    )
    overall = jnp.maximum(cache_peak, self_score)
    keep = jnp.exp(cache_peak - overall)
    fresh = jnp.exp(self_score - overall)
    full_total = cache_total * keep + fresh
    fresh_low = fresh.astype(jnp.bfloat16).astype(jnp.float32)
    full_summed = (
        cache_summed * keep[..., None]
        + fresh_low[..., None] * new_value.astype(jnp.float32)[:, None, :]
    )
    attended = (
        (full_summed / full_total[..., None])
        .astype(jnp.bfloat16)
        .reshape(row_count, local_heads * head_width)
    )
    partial_out = jnp.dot(attended, w_out, preferred_element_type=jnp.float32)
    return lax.psum(partial_out.astype(jnp.bfloat16), "tensor")


def solution(mesh):
    return jax.shard_map(
        local,
        mesh=mesh,
        in_specs=(
            P("dp", None),
            P(),
            P(None, "tensor"),
            P(),
            P("tensor", None),
            P(("dp", "tensor"), None, None),
            P("dp", "tensor"),
            P("dp"),
            P("dp"),
        ),
        out_specs=P("dp", None),
        check_vma=False,
    )
```

profile of v0, /device:TPU:0, one launch (start us, length us, event | category | flops | bytes accessed | tf_op | source)
XLA Modules:
  0.0 160.3 jit_solution(12733547716529152877)
XLA Ops:
  9.9 7.3 %all-to-all-start = ((s32[8,8,2]{1,2,0:T(2,128)}), s32[8,8,2]{1,2,0:T(2,128)S(1)}, u32[]{:S(2)}, u32[]{:S(2)}) async-start(s32[8,8,2]{1,2,0:T(2,128)} %copy.68), calls=%async_computation | async-start | bytes 16384 | tf_op jit(solution)/shard_map/all_to_all | solution.py:97
  19.9 1.6 fusion.25
  21.4 1.6 fusion.27
  23.8 5.4 %all_gather.17 = bf16[64,8,128]{2,0,1:T(8,128)(2,1)S(1)} all-gather(bf16[64,2,128]{2,0,1:T(8,128)(2,1)S(1)} %pad_maximum_fusion), channel_id=1, replica_groups=mesh['dp'=8,'tensor'=4] {'tensor'}, dimensions={1}, use_global_device_ids=true | all-gather | bytes 163840 | tf_op jit(solution)/shard_map/all_gather | solution.py:110
  30.0 6.9 %scatter_fusion = bf16[64,8,128]{2,1,0:T(8,128)(2,1)} fusion(bf16[64,8,128]{2,1,0:T(8,128)(2,1)} %broadcast.188.clone, s32[64]{0:T(128)S(1)} %compare_select_fusion.3, bf16[64,8,128]{2,1,0:T(8,128)(2,1)S(1)} %copy.72), kind=kCustom, calls=%fused_computation.9 | custom fusion | bytes 393472 | tf_op jit(solution)/shard_map/scatter | solution.py:90
  36.9 10.0 %gather_fusion = bf16[128,128,256]{2,1,0:T(8,128)(2,1)} fusion(bf16[128,128,256]{2,1,0:T(8,128)(2,1)} %param.16, s32[1024]{0:T(1024)S(1)} %pad_clamp_fusion.2), kind=kCustom, calls=%fused_computation | custom fusion | bytes 16777728 | tf_op jit(solution)/shard_map/gather | solution.py:118
  46.8 6.0 %all-to-all-start.1 = ((bf16[8,8,8,128]{3,2,1,0:T(8,128)(2,1)}), bf16[8,8,8,128]{3,2,1,0:T(8,128)(2,1)S(1)}, u32[]{:S(2)}, u32[]{:S(2)}) async-start(bf16[8,8,8,128]{3,2,1,0:T(8,128)(2,1)} %bitcast.9), calls=%async_computation.1 | async-start | bytes 262144 | tf_op jit(solution)/shard_map/all_to_all | solution.py:111
  53.8 6.5 %all-to-all-done.1 = bf16[8,8,8,128]{3,2,1,0:T(8,128)(2,1)S(1)} async-done(((bf16[8,8,8,128]{3,2,1,0:T(8,128)(2,1)}), bf16[8,8,8,128]{3,2,1,0:T(8,128)(2,1)S(1)}, u32[]{:S(2)}, u32[]{:S(2)}) %all-to-all-start.1) | async-done | bytes 131104 | tf_op jit(solution)/shard_map/all_to_all | solution.py:111
  60.3 2.5 %scatter_fusion.1 = bf16[64,8,128]{2,1,0:T(8,128)(2,1)S(1)} fusion(bf16[64,8,128]{2,1,0:T(8,128)(2,1)S(1)} %broadcast.188, s32[64]{0:T(128)S(1)} %get-tuple-element.216, bf16[64,8,128]{2,1,0:T(8,128)(2,1)S(1)} %bitcast.88), kind=kCustom, calls=%fused_computation.10 | custom fusion | bytes 393472 | tf_op jit(solution)/shard_map/scatter | solution.py:104
  62.8 3.5 %select_reduce_fusion = (f32[64,8]{1,0:T(8,128)S(1)}, f32[64,8,256]{2,1,0:T(8,128)S(1)}) fusion(pred[64,256]{1,0:T(8,128)(4,1)S(1)} %fusion.24, bf16[64,8,128]{2,1,0:T(8,128)(2,1)S(1)} %scatter_fusion.1, bf16[64,256,256]{2,1,0:T(8,128)(2,1)} %bitcast.82), kind=kOutput, calls=%fused_computation.27 | convolution fusion | flops 33947136 | bytes 4868096 | tf_op jit(solution)/shard_map/vto,vio->vti/dot_general | solution.py:120
  66.3 2.9 %fusion.10 = bf16[64,8,128]{2,1,0:T(8,128)(2,1)S(1)} fusion(bf16[64,256,256]{2,1,0:T(8,128)(2,1)} %bitcast.83, f32[64,8,256]{2,1,0:T(8,128)S(1)} %get-tuple-element.221, f32[64,8]{1,0:T(8,128)S(1)} %get-tuple-element.220, pred[64,256]{1,0:T(8,128)(4,1)S(1)} %fusion.24), kind=kOutput, calls=%fused_computation.25 | convolution fusion | flops 34013184 | bytes 4868096 | tf_op jit(solution)/shard_map/rbi,ril->rbl/dot_general | solution.py:134
  69.6 5.2 %all-gather.4 = bf16[4,64,8]{1,2,0:T(8,128)(2,1)S(1)} all-gather(bf16[1,64,8]{1,2,0:T(8,128)(2,1)S(1)} %copy.75), channel_id=3, replica_groups=mesh['dp'=8,'tensor'=4] {'tensor'}, dimensions={0}, use_global_device_ids=true | all-gather | bytes 5120 | tf_op jit(solution)/shard_map/all_gather | solution.py:13
  74.8 5.1 %all-gather.3 = bf16[4,64,8]{1,2,0:T(8,128)(2,1)S(1)} all-gather(bf16[1,64,8]{1,2,0:T(8,128)(2,1)S(1)} %copy.74), channel_id=2, replica_groups=mesh['dp'=8,'tensor'=4] {'tensor'}, dimensions={0}, use_global_device_ids=true | all-gather | bytes 5120 | tf_op jit(solution)/shard_map/all_gather | solution.py:13
  79.9 7.2 %all-gather.2 = bf16[256,8,128]{2,1,0:T(8,128)(2,1)S(1)} all-gather(bf16[64,8,128]{2,1,0:T(8,128)(2,1)S(1)} %fusion.10), channel_id=4, replica_groups=mesh['dp'=8,'tensor'=4] {'tensor'}, dimensions={0}, use_global_device_ids=true | all-gather | bytes 655360 | tf_op jit(solution)/shard_map/all_gather | solution.py:13
  87.2 1.5 while.19
  90.0 3.3 %all-to-all-start.3 = ((bf16[8,8,8]{2,1,0:T(8,128)(2,1)}), bf16[8,8,8]{2,1,0:T(8,128)(2,1)S(1)}, u32[]{:S(2)}, u32[]{:S(2)}) async-start(bf16[8,8,8]{2,1,0:T(8,128)(2,1)} %bitcast.65), calls=%async_computation.3 | async-start | bytes 32768 | tf_op jit(solution)/shard_map/all_to_all | solution.py:142
  94.7 5.2 %all-to-all-done.3 = bf16[8,8,8]{2,1,0:T(8,128)(2,1)S(1)} async-done(((bf16[8,8,8]{2,1,0:T(8,128)(2,1)}), bf16[8,8,8]{2,1,0:T(8,128)(2,1)S(1)}, u32[]{:S(2)}, u32[]{:S(2)}) %all-to-all-start.3) | async-done | bytes 1056 | tf_op jit(solution)/shard_map/all_to_all | solution.py:142
  99.9 3.3 %all-to-all-start.4 = ((bf16[8,8,8]{2,1,0:T(8,128)(2,1)}), bf16[8,8,8]{2,1,0:T(8,128)(2,1)S(1)}, u32[]{:S(2)}, u32[]{:S(2)}) async-start(bf16[8,8,8]{2,1,0:T(8,128)(2,1)} %bitcast.64), calls=%async_computation.4 | async-start | bytes 32768 | tf_op jit(solution)/shard_map/all_to_all | solution.py:143
  103.3 1.3 gather_fusion.1
  105.2 4.5 %all-to-all-done.4 = bf16[8,8,8]{2,1,0:T(8,128)(2,1)S(1)} async-done(((bf16[8,8,8]{2,1,0:T(8,128)(2,1)}), bf16[8,8,8]{2,1,0:T(8,128)(2,1)S(1)}, u32[]{:S(2)}, u32[]{:S(2)}) %all-to-all-start.4) | async-done | bytes 1056 | tf_op jit(solution)/shard_map/all_to_all | solution.py:143
  109.7 3.4 %all-to-all-start.2 = ((bf16[8,8,8,128]{3,2,1,0:T(8,128)(2,1)}), bf16[8,8,8,128]{3,2,1,0:T(8,128)(2,1)S(1)}, u32[]{:S(2)}, u32[]{:S(2)}) async-start(bf16[8,8,8,128]{3,2,1,0:T(8,128)(2,1)} %bitcast.18), calls=%async_computation.2 | async-start | bytes 262144 | tf_op jit(solution)/shard_map/all_to_all | solution.py:144
  114.4 6.0 %all-to-all-done.2 = bf16[8,8,8,128]{3,2,1,0:T(8,128)(2,1)S(1)} async-done(((bf16[8,8,8,128]{3,2,1,0:T(8,128)(2,1)}), bf16[8,8,8,128]{3,2,1,0:T(8,128)(2,1)S(1)}, u32[]{:S(2)}, u32[]{:S(2)}) %all-to-all-start.2) | async-done | bytes 131104 | tf_op jit(solution)/shard_map/all_to_all | solution.py:144
  122.3 29.6 %all-reduce.2.cloned.1.call-done = bf16[64,1536]{1,0:T(8,128)(2,1)} async-done(((bf16[64,1536]{1,0:T(8,128)(2,1)}), bf16[64,1536]{1,0:T(8,128)(2,1)}) %all-reduce.2.cloned.1.call-update) | async-done | bytes 196624 | tf_op jit(solution)/shard_map/psum | solution.py:171
  151.8 1.6 %copy.131 = bf16[64,1536]{1,0:T(8,128)(2,1)} copy(bf16[64,1536]{1,0:T(8,128)(2,1)} %all-reduce.2.cloned.1.call-done) | data formatting | bytes 393216
  (78 shorter events, 16.8 us)
Async XLA Ops:
  6.5 114.8 %copy-start = (bf16[256,1536]{1,0:T(8,128)(2,1)S(1)}, bf16[256,1536]{1,0:T(8,128)(2,1)}, u32[]{:S(2)}) copy-start(bf16[256,1536]{1,0:T(8,128)(2,1)} %param.15) | copy-start | bytes 2359300
  9.9 37.0 %all-to-all-start = ((s32[8,8,2]{1,2,0:T(2,128)}), s32[8,8,2]{1,2,0:T(2,128)S(1)}, u32[]{:S(2)}, u32[]{:S(2)}) async-start(s32[8,8,2]{1,2,0:T(2,128)} %copy.68), calls=%async_computation | async-start | bytes 16384 | tf_op jit(solution)/shard_map/all_to_all | solution.py:97
  46.8 13.5 %all-to-all-start.1 = ((bf16[8,8,8,128]{3,2,1,0:T(8,128)(2,1)}), bf16[8,8,8,128]{3,2,1,0:T(8,128)(2,1)S(1)}, u32[]{:S(2)}, u32[]{:S(2)}) async-start(bf16[8,8,8,128]{3,2,1,0:T(8,128)(2,1)} %bitcast.9), calls=%async_computation.1 | async-start | bytes 262144 | tf_op jit(solution)/shard_map/all_to_all | solution.py:111
  90.0 9.9 %all-to-all-start.3 = ((bf16[8,8,8]{2,1,0:T(8,128)(2,1)}), bf16[8,8,8]{2,1,0:T(8,128)(2,1)S(1)}, u32[]{:S(2)}, u32[]{:S(2)}) async-start(bf16[8,8,8]{2,1,0:T(8,128)(2,1)} %bitcast.65), calls=%async_computation.3 | async-start | bytes 32768 | tf_op jit(solution)/shard_map/all_to_all | solution.py:142
  99.9 9.9 %all-to-all-start.4 = ((bf16[8,8,8]{2,1,0:T(8,128)(2,1)}), bf16[8,8,8]{2,1,0:T(8,128)(2,1)S(1)}, u32[]{:S(2)}, u32[]{:S(2)}) async-start(bf16[8,8,8]{2,1,0:T(8,128)(2,1)} %bitcast.64), calls=%async_computation.4 | async-start | bytes 32768 | tf_op jit(solution)/shard_map/all_to_all | solution.py:143
  109.7 10.7 %all-to-all-start.2 = ((bf16[8,8,8,128]{3,2,1,0:T(8,128)(2,1)}), bf16[8,8,8,128]{3,2,1,0:T(8,128)(2,1)S(1)}, u32[]{:S(2)}, u32[]{:S(2)}) async-start(bf16[8,8,8,128]{3,2,1,0:T(8,128)(2,1)} %bitcast.18), calls=%async_computation.2 | async-start | bytes 262144 | tf_op jit(solution)/shard_map/all_to_all | solution.py:144
  113.1 38.7 %all-reduce.2.cloned.1.call-start = ((), (), s32[]{:S(2)}) async-start(), calls=%async_computation.5 | async-start | bytes 393216 | tf_op jit(solution)/shard_map/psum | solution.py:171
Sparse Core Ops, SparseCore 0:
  122.4 29.3 all-reduce.1
where the time goes:
time: 161 us; the launch traced here: 160 us
  waiting for transfers between devices  51.7 us (32%)
  local copies, waits for them, and re-layouts  31.7 us (20%)
  starting transfers between devices  23.4 us (15%)
  blocking collectives  23 us (14%)
  between operations  13.6 us (8%)
  matrix products  10.6 us (7%)
  other arithmetic  6.19 us (4%)
    psum x1, waiting for transfers between devices, local(): return lax.psum(partial_out.astype(jnp.bfloat16), 'tensor')  29.6 us
    all_gather x3, blocking collectives, combined_all(): lax.all_gather(a.astype(kind), axis)  17.6 us
    gather x1, local copies, waits for them, and re-layouts, local(): kv_pool[page_table].reshape(row_count, page_rows * page_len, 2 * head_width)  9.96 us
    scatter x2, local copies, waits for them, and re-layouts, to_buffer(): filled = empty.at[place].set(values)  7.66 us
    all_to_all x1, starting transfers between devices, local(): lax.all_to_all(tags, 'dp', split_axis=0, concat_axis=0, tiled=True)  7.28 us
    all_to_all x1, waiting for transfers between devices, local(): lax.all_to_all(to_buffer(full_query), 'dp', split_axis=0, concat_axis=0,...  6.47 us
    all_to_all x1, waiting for transfers between devices, local(): lax.all_to_all(as_sent(expand(merged[2])), 'dp', split_axis=0, concat_axi...  6.02 us
    all_to_all x1, starting transfers between devices, local(): lax.all_to_all(to_buffer(full_query), 'dp', split_axis=0, concat_axis=0,...  6 us
  transfers between devices with their start and end apart: 6, of which 5 were waited for; matrix products, arithmetic and copies ran while one was open for 19% of the time, Pallas kernels for 0%

commit v1 on v0

--- a/solution.py
+++ b/solution.py
@@ -6,6 +6,18 @@
 masked_score = -1e30
 norm_eps = 1e-06
 rotary_base = 10000.0
+
+
+def exchange_directly(shard, axis, split, join):
+    ways, here = (lax.axis_size(axis), lax.axis_index(axis))
+    width = shard.shape[split] // ways
+    turned = jnp.roll(shard, -here * width, axis=split)
+    got = [lax.slice_in_dim(turned, 0, width, axis=split)]
+    for far in range(1, ways):
+        sent = lax.slice_in_dim(turned, far * width, (far + 1) * width, axis=split)
+        got.append(lax.ppermute(sent, axis, [(d, (d + far) % ways) for d in range(ways)]))
+    line = jnp.concatenate(got[::-1], axis=join)
+    return jnp.roll(line, (here + 1) * got[0].shape[join], axis=join)
 
 
 def combined_all(array, axis, join):
@@ -94,7 +106,7 @@
         return values.reshape((slots_all,) + values.shape[2:])[place]
 
     tags = to_buffer(jnp.stack([positions, local_slot + 1], axis=1))
-    tags = lax.all_to_all(tags, "dp", split_axis=0, concat_axis=0, tiled=True).reshape(slots_all, 2)
+    tags = exchange_directly(tags, "dp", 0, 0).reshape(slots_all, 2)
     served_slot = tags[:, 1] - 1
     scatter_slot = jnp.where(served_slot < 0, row_count, served_slot)
     gather_slot = jnp.maximum(served_slot, 0)

time: 161 us -> 164 us (1.019)
  starting transfers between devices: 23.4 us -> 31.7 us
  waiting for transfers between devices: 51.7 us -> 47.4 us
    ppermute x0 -> x7, starting transfers between devices: none -> 16.2 us  [exchange_directly(): lax.ppermute(sent, axis, [(d, (d + far) % ways) for d in range(ways)])]
    all_to_all x1 -> x0, starting transfers between devices: 7.28 us -> none  [local(): lax.all_to_all(tags, 'dp', split_axis=0, concat_axis=0, tiled=True)]
    all_to_all x1, waiting for transfers between devices: 6.47 us -> 0.01 us  [local(): lax.all_to_all(to_buffer(full_query), 'dp', split_axis=0, concat_axis=0,...]
    all_to_all x1, starting transfers between devices: 6 us -> 3.37 us  [local(): lax.all_to_all(to_buffer(full_query), 'dp', split_axis=0, concat_axis=0,...]
    ppermute x0 -> x7, waiting for transfers between devices: none -> 2.11 us  [exchange_directly(): lax.ppermute(sent, axis, [(d, (d + far) % ways) for d in range(ways)])]
    all_to_all x1, starting transfers between devices: 3.34 us -> 5.43 us  [local(): lax.all_to_all(as_sent(expand(merged[0])), 'dp', split_axis=0, concat_axi...]
  transfers between devices with their start and end apart: 6 -> 12, of which waited for: 5 -> 5; matrix products, arithmetic and copies ran while one was open for 19% -> 18% of each run, Pallas kernels for 0% -> 0%
where the time goes in v1:
time: 164 us; the launch traced here: 163 us
  waiting for transfers between devices  47.4 us (29%)
  starting transfers between devices  31.7 us (19%)
  local copies, waits for them, and re-layouts  31.2 us (19%)
  blocking collectives  23 us (14%)
  between operations  13.7 us (8%)
  matrix products  10.6 us (6%)
  other arithmetic  5.56 us (3%)
    psum x1, waiting for transfers between devices, local(): return lax.psum(partial_out.astype(jnp.bfloat16), 'tensor')  29.6 us
    all_gather x3, blocking collectives, combined_all(): lax.all_gather(a.astype(kind), axis)  17.6 us
    ppermute x7, starting transfers between devices, exchange_directly(): lax.ppermute(sent, axis, [(d, (d + far) % ways) for d in range(ways)])  16.2 us
    gather x1, local copies, waits for them, and re-layouts, local(): kv_pool[page_table].reshape(row_count, page_rows * page_len, 2 * head_width)  9.96 us
    scatter x2, local copies, waits for them, and re-layouts, to_buffer(): filled = empty.at[place].set(values)  7.66 us
    all_to_all x1, waiting for transfers between devices, local(): lax.all_to_all(as_sent(expand(merged[2])), 'dp', split_axis=0, concat_axi...  5.95 us
    all_to_all x1, starting transfers between devices, local(): lax.all_to_all(as_sent(expand(merged[0])), 'dp', split_axis=0, concat_axi...  5.43 us
    all_gather x1, blocking collectives, local(): full_query = lax.all_gather(query, 'tensor', axis=1, tiled=True)  5.43 us
  transfers between devices with their start and end apart: 12, of which 5 were waited for; matrix products, arithmetic and copies ran while one was open for 18% of the time, Pallas kernels for 0%

profile of v1, /device:TPU:0, one launch (start us, length us, event | category | flops | bytes accessed | tf_op | source)
XLA Modules:
  0.0 163.2 jit_solution(13503259166468704683)
XLA Ops:
  9.3 3.0 %collective-permute-start.6 = (s32[1,8,2]{1,0,2:T(1,128)S(1)}, s32[1,8,2]{1,0,2:T(1,128)S(1)}, u32[]{:S(2)}, u32[]{:S(2)}) collective-permute-start(s32[1,8,2]{1,0,2:T(1,128)S(1)} %get-tuple-element.214), channel_id=1, source_target_pairs={{0,4},{4,8},{8,12},{12,16},{16,20},{20,24},{24,28},{28,0},{1,5},{5... | collective-permute-start | bytes 200 | tf_op jit(solution)/shard_map/ppermute | solution.py:18
  12.4 1.6 collective-permute-start.5
  13.9 2.5 %collective-permute-start.4 = (s32[1,8,2]{1,0,2:T(1,128)S(1)}, s32[1,8,2]{1,0,2:T(1,128)S(1)}, u32[]{:S(2)}, u32[]{:S(2)}) collective-permute-start(s32[1,8,2]{1,0,2:T(1,128)S(1)} %get-tuple-element.216), channel_id=1, source_target_pairs={{0,12},{4,16},{8,20},{12,24},{16,28},{20,0},{24,4},{28,8},{1,13},{... | collective-permute-start | bytes 200 | tf_op jit(solution)/shard_map/ppermute | solution.py:18
  17.7 2.6 %collective-permute-start.2 = (s32[1,8,2]{1,0,2:T(1,128)S(1)}, s32[1,8,2]{1,0,2:T(1,128)S(1)}, u32[]{:S(2)}, u32[]{:S(2)}) collective-permute-start(s32[1,8,2]{1,0,2:T(1,128)S(1)} %get-tuple-element.218), channel_id=1, source_target_pairs={{0,20},{4,24},{8,28},{12,0},{16,4},{20,8},{24,12},{28,16},{1,21},{... | collective-permute-start | bytes 200 | tf_op jit(solution)/shard_map/ppermute | solution.py:18
  25.7 5.4 %all_gather.17 = bf16[64,8,128]{2,0,1:T(8,128)(2,1)S(1)} all-gather(bf16[64,2,128]{2,0,1:T(8,128)(2,1)S(1)} %pad_maximum_fusion), channel_id=1, replica_groups=mesh['dp'=8,'tensor'=4] {'tensor'}, dimensions={1}, use_global_device_ids=true | all-gather | bytes 163840 | tf_op jit(solution)/shard_map/all_gather | solution.py:122
  31.9 6.9 %scatter_fusion = bf16[64,8,128]{2,1,0:T(8,128)(2,1)} fusion(bf16[64,8,128]{2,1,0:T(8,128)(2,1)} %broadcast.189.clone, s32[64]{0:T(128)S(1)} %compare_select_fusion.3, bf16[64,8,128]{2,1,0:T(8,128)(2,1)S(1)} %copy.66), kind=kCustom, calls=%fused_computation.9 | custom fusion | bytes 393472 | tf_op jit(solution)/shard_map/scatter | solution.py:102
  38.8 3.4 %all-to-all-start = ((bf16[8,8,8,128]{3,2,1,0:T(8,128)(2,1)}), bf16[8,8,8,128]{3,2,1,0:T(8,128)(2,1)S(1)}, u32[]{:S(2)}, u32[]{:S(2)}) async-start(bf16[8,8,8,128]{3,2,1,0:T(8,128)(2,1)} %bitcast.9), calls=%async_computation | async-start | bytes 262144 | tf_op jit(solution)/shard_map/all_to_all | solution.py:123
  42.8 10.0 %gather_fusion = bf16[128,128,256]{2,1,0:T(8,128)(2,1)} fusion(bf16[128,128,256]{2,1,0:T(8,128)(2,1)} %param.18, s32[1024]{0:T(1024)S(1)} %pad_clamp_fusion.2), kind=kCustom, calls=%fused_computation | custom fusion | bytes 16777728 | tf_op jit(solution)/shard_map/gather | solution.py:130
  52.8 3.7 %collective-permute-start.1 = (s32[1,8,2]{1,0,2:T(1,128)S(1)}, s32[1,8,2]{1,0,2:T(1,128)S(1)}, u32[]{:S(2)}, u32[]{:S(2)}) collective-permute-start(s32[1,8,2]{1,0,2:T(1,128)S(1)} %get-tuple-element.219), channel_id=1, source_target_pairs={{0,24},{4,28},{8,0},{12,4},{16,8},{20,12},{24,16},{28,20},{1,25},{... | collective-permute-start | bytes 200 | tf_op jit(solution)/shard_map/ppermute | solution.py:18
  58.0 2.1 %collective-permute-done = s32[1,8,2]{1,0,2:T(1,128)S(1)} collective-permute-done((s32[1,8,2]{1,0,2:T(1,128)S(1)}, s32[1,8,2]{1,0,2:T(1,128)S(1)}, u32[]{:S(2)}, u32[]{:S(2)}) %collective-permute-start) | collective-permute-done | bytes 96 | tf_op jit(solution)/shard_map/ppermute | solution.py:18
  61.2 2.5 %scatter_fusion.1 = bf16[64,8,128]{2,1,0:T(8,128)(2,1)S(1)} fusion(bf16[64,8,128]{2,1,0:T(8,128)(2,1)S(1)} %broadcast.189, s32[64]{0:T(128)S(1)} %get-tuple-element.225, bf16[64,8,128]{2,1,0:T(8,128)(2,1)S(1)} %bitcast.87), kind=kCustom, calls=%fused_computation.10 | custom fusion | bytes 393472 | tf_op jit(solution)/shard_map/scatter | solution.py:116
  63.6 3.5 %select_reduce_fusion = (f32[64,8]{1,0:T(8,128)S(1)}, f32[64,8,256]{2,1,0:T(8,128)S(1)}) fusion(pred[64,256]{1,0:T(8,128)(4,1)S(1)} %fusion.24, bf16[64,8,128]{2,1,0:T(8,128)(2,1)S(1)} %scatter_fusion.1, bf16[64,256,256]{2,1,0:T(8,128)(2,1)} %bitcast.82), kind=kOutput, calls=%fused_computation.27 | convolution fusion | flops 33947136 | bytes 4868096 | tf_op jit(solution)/shard_map/vto,vio->vti/dot_general | solution.py:132
  67.1 2.9 %fusion.10 = bf16[64,8,128]{2,1,0:T(8,128)(2,1)S(1)} fusion(bf16[64,256,256]{2,1,0:T(8,128)(2,1)} %bitcast.83, f32[64,8,256]{2,1,0:T(8,128)S(1)} %get-tuple-element.230, f32[64,8]{1,0:T(8,128)S(1)} %get-tuple-element.229, pred[64,256]{1,0:T(8,128)(4,1)S(1)} %fusion.24), kind=kOutput, calls=%fused_computation.25 | convolution fusion | flops 34013184 | bytes 4868096 | tf_op jit(solution)/shard_map/rbi,ril->rbl/dot_general | solution.py:146
  70.4 5.2 %all-gather.4 = bf16[4,64,8]{1,2,0:T(8,128)(2,1)S(1)} all-gather(bf16[1,64,8]{1,2,0:T(8,128)(2,1)S(1)} %copy.69), channel_id=3, replica_groups=mesh['dp'=8,'tensor'=4] {'tensor'}, dimensions={0}, use_global_device_ids=true | all-gather | bytes 5120 | tf_op jit(solution)/shard_map/all_gather | solution.py:25
  75.6 5.1 %all-gather.3 = bf16[4,64,8]{1,2,0:T(8,128)(2,1)S(1)} all-gather(bf16[1,64,8]{1,2,0:T(8,128)(2,1)S(1)} %copy.68), channel_id=2, replica_groups=mesh['dp'=8,'tensor'=4] {'tensor'}, dimensions={0}, use_global_device_ids=true | all-gather | bytes 5120 | tf_op jit(solution)/shard_map/all_gather | solution.py:25
  80.8 7.2 %all-gather.2 = bf16[256,8,128]{2,1,0:T(8,128)(2,1)S(1)} all-gather(bf16[64,8,128]{2,1,0:T(8,128)(2,1)S(1)} %fusion.10), channel_id=4, replica_groups=mesh['dp'=8,'tensor'=4] {'tensor'}, dimensions={0}, use_global_device_ids=true | all-gather | bytes 655360 | tf_op jit(solution)/shard_map/all_gather | solution.py:25
  90.8 5.4 %all-to-all-start.2 = ((bf16[8,8,8]{2,1,0:T(8,128)(2,1)}), bf16[8,8,8]{2,1,0:T(8,128)(2,1)S(1)}, u32[]{:S(2)}, u32[]{:S(2)}) async-start(bf16[8,8,8]{2,1,0:T(8,128)(2,1)} %bitcast.65), calls=%async_computation.2 | async-start | bytes 32768 | tf_op jit(solution)/shard_map/all_to_all | solution.py:154
  97.6 5.2 %all-to-all-done.2 = bf16[8,8,8]{2,1,0:T(8,128)(2,1)S(1)} async-done(((bf16[8,8,8]{2,1,0:T(8,128)(2,1)}), bf16[8,8,8]{2,1,0:T(8,128)(2,1)S(1)}, u32[]{:S(2)}, u32[]{:S(2)}) %all-to-all-start.2) | async-done | bytes 1056 | tf_op jit(solution)/shard_map/all_to_all | solution.py:154
  102.8 3.3 %all-to-all-start.3 = ((bf16[8,8,8]{2,1,0:T(8,128)(2,1)}), bf16[8,8,8]{2,1,0:T(8,128)(2,1)S(1)}, u32[]{:S(2)}, u32[]{:S(2)}) async-start(bf16[8,8,8]{2,1,0:T(8,128)(2,1)} %bitcast.64), calls=%async_computation.3 | async-start | bytes 32768 | tf_op jit(solution)/shard_map/all_to_all | solution.py:155
  108.2 4.5 %all-to-all-done.3 = bf16[8,8,8]{2,1,0:T(8,128)(2,1)S(1)} async-done(((bf16[8,8,8]{2,1,0:T(8,128)(2,1)}), bf16[8,8,8]{2,1,0:T(8,128)(2,1)S(1)}, u32[]{:S(2)}, u32[]{:S(2)}) %all-to-all-start.3) | async-done | bytes 1056 | tf_op jit(solution)/shard_map/all_to_all | solution.py:155
  112.7 3.4 %all-to-all-start.1 = ((bf16[8,8,8,128]{3,2,1,0:T(8,128)(2,1)}), bf16[8,8,8,128]{3,2,1,0:T(8,128)(2,1)S(1)}, u32[]{:S(2)}, u32[]{:S(2)}) async-start(bf16[8,8,8,128]{3,2,1,0:T(8,128)(2,1)} %bitcast.18), calls=%async_computation.1 | async-start | bytes 262144 | tf_op jit(solution)/shard_map/all_to_all | solution.py:156
  117.4 5.9 %all-to-all-done.1 = bf16[8,8,8,128]{3,2,1,0:T(8,128)(2,1)S(1)} async-done(((bf16[8,8,8,128]{3,2,1,0:T(8,128)(2,1)}), bf16[8,8,8,128]{3,2,1,0:T(8,128)(2,1)S(1)}, u32[]{:S(2)}, u32[]{:S(2)}) %all-to-all-start.1) | async-done | bytes 131104 | tf_op jit(solution)/shard_map/all_to_all | solution.py:156
  125.2 29.6 %all-reduce.2.cloned.1.call-done = bf16[64,1536]{1,0:T(8,128)(2,1)} async-done(((bf16[64,1536]{1,0:T(8,128)(2,1)}), bf16[64,1536]{1,0:T(8,128)(2,1)}) %all-reduce.2.cloned.1.call-update) | async-done | bytes 196624 | tf_op jit(solution)/shard_map/psum | solution.py:183
  154.8 1.6 copy.134
  (93 shorter events, 24.3 us)
Async XLA Ops:
  6.5 117.7 %copy-start = (bf16[256,1536]{1,0:T(8,128)(2,1)S(1)}, bf16[256,1536]{1,0:T(8,128)(2,1)}, u32[]{:S(2)}) copy-start(bf16[256,1536]{1,0:T(8,128)(2,1)} %param.17) | copy-start | bytes 2359300
  9.3 43.4 %collective-permute-start.6 = (s32[1,8,2]{1,0,2:T(1,128)S(1)}, s32[1,8,2]{1,0,2:T(1,128)S(1)}, u32[]{:S(2)}, u32[]{:S(2)}) collective-permute-start(s32[1,8,2]{1,0,2:T(1,128)S(1)} %get-tuple-element.214), channel_id=1, source_target_pairs={{0,4},{4,8},{8,12},{12,16},{16,20},{20,24},{24,28},{28,0},{1,5},{5... | collective-permute-start | bytes 200 | tf_op jit(solution)/shard_map/ppermute | solution.py:18
  12.4 44.1 %collective-permute-start.5 = (s32[1,8,2]{1,0,2:T(1,128)S(1)}, s32[1,8,2]{1,0,2:T(1,128)S(1)}, u32[]{:S(2)}, u32[]{:S(2)}) collective-permute-start(s32[1,8,2]{1,0,2:T(1,128)S(1)} %get-tuple-element.215), channel_id=1, source_target_pairs={{0,8},{4,12},{8,16},{12,20},{16,24},{20,28},{24,0},{28,4},{1,9},{5... | collective-permute-start | bytes 200 | tf_op jit(solution)/shard_map/ppermute | solution.py:18
  13.9 44.0 %collective-permute-start.4 = (s32[1,8,2]{1,0,2:T(1,128)S(1)}, s32[1,8,2]{1,0,2:T(1,128)S(1)}, u32[]{:S(2)}, u32[]{:S(2)}) collective-permute-start(s32[1,8,2]{1,0,2:T(1,128)S(1)} %get-tuple-element.216), channel_id=1, source_target_pairs={{0,12},{4,16},{8,20},{12,24},{16,28},{20,0},{24,4},{28,8},{1,13},{... | collective-permute-start | bytes 200 | tf_op jit(solution)/shard_map/ppermute | solution.py:18
  16.5 41.5 %collective-permute-start.3 = (s32[1,8,2]{1,0,2:T(1,128)S(1)}, s32[1,8,2]{1,0,2:T(1,128)S(1)}, u32[]{:S(2)}, u32[]{:S(2)}) collective-permute-start(s32[1,8,2]{1,0,2:T(1,128)S(1)} %get-tuple-element.217), channel_id=1, source_target_pairs={{0,16},{4,20},{8,24},{12,28},{16,0},{20,4},{24,8},{28,12},{1,17},{... | collective-permute-start | bytes 200 | tf_op jit(solution)/shard_map/ppermute | solution.py:18
  17.7 40.2 %collective-permute-start.2 = (s32[1,8,2]{1,0,2:T(1,128)S(1)}, s32[1,8,2]{1,0,2:T(1,128)S(1)}, u32[]{:S(2)}, u32[]{:S(2)}) collective-permute-start(s32[1,8,2]{1,0,2:T(1,128)S(1)} %get-tuple-element.218), channel_id=1, source_target_pairs={{0,20},{4,24},{8,28},{12,0},{16,4},{20,8},{24,12},{28,16},{1,21},{... | collective-permute-start | bytes 200 | tf_op jit(solution)/shard_map/ppermute | solution.py:18
  38.8 22.3 %all-to-all-start = ((bf16[8,8,8,128]{3,2,1,0:T(8,128)(2,1)}), bf16[8,8,8,128]{3,2,1,0:T(8,128)(2,1)S(1)}, u32[]{:S(2)}, u32[]{:S(2)}) async-start(bf16[8,8,8,128]{3,2,1,0:T(8,128)(2,1)} %bitcast.9), calls=%async_computation | async-start | bytes 262144 | tf_op jit(solution)/shard_map/all_to_all | solution.py:123
  52.8 5.2 %collective-permute-start.1 = (s32[1,8,2]{1,0,2:T(1,128)S(1)}, s32[1,8,2]{1,0,2:T(1,128)S(1)}, u32[]{:S(2)}, u32[]{:S(2)}) collective-permute-start(s32[1,8,2]{1,0,2:T(1,128)S(1)} %get-tuple-element.219), channel_id=1, source_target_pairs={{0,24},{4,28},{8,0},{12,4},{16,8},{20,12},{24,16},{28,20},{1,25},{... | collective-permute-start | bytes 200 | tf_op jit(solution)/shard_map/ppermute | solution.py:18
  56.5 3.6 %collective-permute-start = (s32[1,8,2]{1,0,2:T(1,128)S(1)}, s32[1,8,2]{1,0,2:T(1,128)S(1)}, u32[]{:S(2)}, u32[]{:S(2)}) collective-permute-start(s32[1,8,2]{1,0,2:T(1,128)S(1)} %get-tuple-element.220), channel_id=1, source_target_pairs={{0,28},{4,0},{8,4},{12,8},{16,12},{20,16},{24,20},{28,24},{1,29},{... | collective-permute-start | bytes 200 | tf_op jit(solution)/shard_map/ppermute | solution.py:18
  90.8 12.0 %all-to-all-start.2 = ((bf16[8,8,8]{2,1,0:T(8,128)(2,1)}), bf16[8,8,8]{2,1,0:T(8,128)(2,1)S(1)}, u32[]{:S(2)}, u32[]{:S(2)}) async-start(bf16[8,8,8]{2,1,0:T(8,128)(2,1)} %bitcast.65), calls=%async_computation.2 | async-start | bytes 32768 | tf_op jit(solution)/shard_map/all_to_all | solution.py:154
  102.8 9.8 %all-to-all-start.3 = ((bf16[8,8,8]{2,1,0:T(8,128)(2,1)}), bf16[8,8,8]{2,1,0:T(8,128)(2,1)S(1)}, u32[]{:S(2)}, u32[]{:S(2)}) async-start(bf16[8,8,8]{2,1,0:T(8,128)(2,1)} %bitcast.64), calls=%async_computation.3 | async-start | bytes 32768 | tf_op jit(solution)/shard_map/all_to_all | solution.py:155
  112.7 10.7 %all-to-all-start.1 = ((bf16[8,8,8,128]{3,2,1,0:T(8,128)(2,1)}), bf16[8,8,8,128]{3,2,1,0:T(8,128)(2,1)S(1)}, u32[]{:S(2)}, u32[]{:S(2)}) async-start(bf16[8,8,8,128]{3,2,1,0:T(8,128)(2,1)} %bitcast.18), calls=%async_computation.1 | async-start | bytes 262144 | tf_op jit(solution)/shard_map/all_to_all | solution.py:156
  116.1 38.7 %all-reduce.2.cloned.1.call-start = ((), (), s32[]{:S(2)}) async-start(), calls=%async_computation.4 | async-start | bytes 393216 | tf_op jit(solution)/shard_map/psum | solution.py:183
Sparse Core Ops, SparseCore 0:
  125.3 29.3 all-reduce.1
